TPU v7x, 128 devices: a whole 4x4x4 slice. The times are simulated.
128 devices in a mesh: row: 8 (over z, core), col: 16 (over y, x).
Axes of the slice: x: 4, y: 4, z: 4, core: 2. Of those that a mesh axis runs over, the one named last changes fastest.
Arguments:
- snapshots: bfloat16 [4096, 32768], P('row', 'col'), may hold values from -14 to 14
- neighbours: int32 [4096, 128], P('row'), may hold values from 0 to 4095, all different within a row
- start_basis: float32 [32, 4096], replicated, may hold values from -6 to 6
Outputs:
- basis: float32 [32, 4096], P(None, 'row')
- rayleigh: float32 [32, 32], replicated
Inputs may be any that keep to these rules, and one draw needn't show every extreme that they name: `neighbours`: each row names 128 different snapshots.
All inputs are finite; a program needn't handle non-finite values.
Results may differ from a plain program's by a relative error of at most 0.00145.
Values may be sent and summed in bfloat16 or wider, within the bound.
No kernel may reach another device: no remote copies, remote signals or barrier semaphores. Data moves between devices by JAX's collectives and lax.ppermute only.
A program may use at most 128 MiB of HBM per device.

v0:
```python
import math
import jax
import jax.numpy as jnp
from jax import lax
from jax.sharding import PartitionSpec as P

FEATURES = 32768
LAGS = 64
ITERS = 2


def global_sum(value):
    return lax.psum(value, ("row", "col"))


def collect(columns):
    return lax.all_gather(columns, ("row", "col"), axis=1, tiled=True)


def shards(snapshots, neighbours, start_basis):
    row_count = lax.axis_size("row")
    col_count = lax.axis_size("col")
    row_at = lax.axis_index("row")
    col_at = lax.axis_index("col")
    lag_count = LAGS
    whole = lax.all_gather(snapshots, "row", axis=0, tiled=True)
    snap_count = whole.shape[0]
    feat_width = whole.shape[1]
    col_block = snap_count // col_count
    row_block = snapshots.shape[0]
    squares = jnp.sum(jnp.square(whole.astype(jnp.float32)), axis=1)
    padded_rows = jnp.concatenate([jnp.zeros((lag_count, feat_width), whole.dtype), whole], 0)
    padded_norms = jnp.concatenate([jnp.zeros((lag_count,), jnp.float32), squares], 0)
    row_start = row_at * row_block
    ext_rows = lax.dynamic_slice_in_dim(padded_rows, row_start, row_block + lag_count, 0)
    ext_norms = lax.dynamic_slice_in_dim(padded_norms, row_start, row_block + lag_count, 0)
    row_times = row_start - lag_count + jnp.arange(row_block + lag_count, dtype=jnp.int32)
    span = col_block + lag_count
    blocks = whole.reshape(col_count, col_block, feat_width)
    earlier = jnp.concatenate(
        [jnp.zeros((1, lag_count, feat_width), whole.dtype), blocks[:-1, col_block - lag_count :]],
        0,
    )
    source_rows = jnp.concatenate([earlier, blocks], 1).reshape(col_count * span, feat_width)
    norm_blocks = squares.reshape(col_count, col_block)
    norm_earlier = jnp.concatenate(
        [jnp.zeros((1, lag_count), jnp.float32), norm_blocks[:-1, col_block - lag_count :]], 0
    )
    source_norms = jnp.concatenate([norm_earlier, norm_blocks], 1).reshape(col_count * span)
    virtual = jnp.arange(span * lax.axis_size("col"), dtype=jnp.int32)
    times = virtual // span * col_block + virtual % span - lag_count
    inner = lax.dot_general(
        source_rows, ext_rows, (((1,), (1,)), ((), ())), preferred_element_type=jnp.float32
    )
    term = source_norms[:, None] + ext_norms[None, :] - 2.0 * inner
    keep = (times >= 0)[:, None] & (row_times >= 0)[None, :]
    tile = lax.psum_scatter(
        jnp.where(keep, term, 0.0).astype(jnp.bfloat16), "col", scatter_dimension=0, tiled=True
    ).astype(jnp.float32)
    window = 1
    while window < lag_count:
        tile = tile[window:, window:] + tile[:-window, :-window]
        window = window * 2
    lagged = tile[1:, 1:]
    step_rows = math.gcd(row_block, 16)
    block_count = row_block // step_rows
    slot_count = neighbours.shape[1]
    offset = neighbours - col_at * col_block
    inside = (offset >= 0) & (offset < col_block)
    tile_positions = jnp.arange(col_block, dtype=jnp.int32)

    def pick_block(pair):
        offs, lag_rows = pair
        match = offs[:, :, None] == tile_positions[None, None, :]
        return jnp.sum(jnp.where(match, lag_rows[:, None, :], 0.0), axis=2)

    chosen = lax.map(
        pick_block,
        (
            offset.reshape(block_count, step_rows, slot_count),
            lagged.T.reshape(block_count, step_rows, col_block),
        ),
    )
    chosen = chosen.reshape(row_block, slot_count)
    kernel_part = jnp.where(inside, 1.0 / (1.0 + chosen / (LAGS * FEATURES)), 0.0)
    slot_kernel = lax.psum(kernel_part, "col")
    mass = jnp.sum(slot_kernel, axis=1)
    markov = slot_kernel / mass[:, None]
    snap_positions = jnp.arange(snap_count, dtype=jnp.int32)

    def operator_block(pair):
        ids, weights = pair
        match = ids[:, :, None] == snap_positions[None, None, :]
        return jnp.sum(jnp.where(match, weights[:, :, None], 0.0), axis=1)

    transition = lax.map(
        operator_block,
        (
            neighbours.reshape(block_count, step_rows, slot_count),
            markov.reshape(block_count, step_rows, slot_count),
        ),
    )
    transition = transition.reshape(row_block, snap_count)
    piece_width = snap_count // (row_count * col_count)

    def apply_rows(basis_rows):
        return lax.dot_general(
            basis_rows,
            transition,
            (((1,), (1,)), ((), ())),
            precision=lax.Precision.HIGHEST,
            preferred_element_type=jnp.float32,
        )

    def own_piece(image):
        return lax.dynamic_slice_in_dim(image, col_at * piece_width, piece_width, 1)

    basis = start_basis
    for step in range(ITERS):
        piece = own_piece(apply_rows(basis))
        partial_gram = jnp.dot(
            piece, piece.T, precision=lax.Precision.HIGHEST, preferred_element_type=jnp.float32
        )
        gram_small = global_sum(partial_gram) / snap_count
        lower = jnp.linalg.cholesky(gram_small)
        basis = collect(jax.scipy.linalg.solve_triangular(lower, piece, lower=True))
    image_piece = own_piece(apply_rows(basis))
    basis_piece = lax.dynamic_slice_in_dim(
        basis, (row_at * col_count + col_at) * piece_width, piece_width, 1
    )
    partial_ray = jnp.dot(
        basis_piece,
        image_piece.T,
        precision=lax.Precision.HIGHEST,
        preferred_element_type=jnp.float32,
    )
    rayleigh = global_sum(partial_ray) / snap_count
    basis_rows = lax.dynamic_slice_in_dim(basis, row_start, row_block, 1)
    return (basis_rows, rayleigh)


def solution(mesh):
    placed = (P("row", "col"), P("row", None), P())
    return jax.shard_map(
        shards, mesh=mesh, in_specs=placed, out_specs=(P(None, "row"), P()), check_vma=False
    )
```

profile of v0, /device:TPU:1, one launch (start us, length us, event | category | flops | bytes accessed | tf_op | source)
XLA Modules:
  0.0 1007.9 jit_solution(16402256858035387622)
XLA Ops:
  8.0 90.6 %all-gather.2.cloned.1.call-done = bf16[4096,2048]{1,0:T(8,128)(2,1)} async-done(((bf16[512,2048]{1,0:T(8,128)(2,1)}), bf16[4096,2048]{1,0:T(8,128)(2,1)}) %all-gather.2.cloned.1.call-update) | async-done | bytes 16777232 | tf_op jit(solution)/shard_map/all_gather | solution.py:26
  108.7 21.4 %fusion.5 = bf16[16,320,2048]{2,1,0:T(8,128)(2,1)} fusion(bf16[15,64,2048]{2,1,0:T(8,128)(2,1)S(1)} %slice.69, bf16[16,256,2048]{2,1,0:T(8,128)(2,1)} %bitcast.64), kind=kLoop, calls=%fused_computation.15 | loop fusion | flops 62914560 | bytes 41680896 | tf_op jit(solution)/shard_map/concatenate | solution.py:44
  130.2 23.8 %select_convert_fusion = bf16[5120,576]{1,0:T(8,128)(2,1)} fusion(bf16[5120,2048]{1,0:T(8,128)(2,1)} %bitcast.70, f32[576]{0:T(1024)S(1)} %pad_dynamic-slice_fusion.2, f32[5120]{0:T(1024)S(1)} %add.130, pred[576]{0:T(1024)(128)(4,1)S(1)} %add_compare_fusion, pred[5120]{0:T(1024)(128)(4,1)S(1)} %fusion.17, s32[]{:T(128)S(6)} %select_n.56, ...), kind=kOutput, calls=%fused_computation.17 | convolution fusion | flops 12097290240 | bytes 43675460 | tf_op jit(solution)/shard_map/dot_general | solution.py:52
  154.1 80.7 %reduce-scatter.2.cloned.1.call-done = bf16[320,576]{1,0:T(8,128)(2,1)} async-done(((bf16[5120,576]{1,0:T(8,128)(2,1)}), bf16[320,576]{1,0:T(8,128)(2,1)}) %reduce-scatter.2.cloned.1.call-update) | async-done | bytes 368656 | tf_op jit(solution)/shard_map/reduce_scatter | solution.py:57
  238.1 28.1 %while.22 = (s32[]{:T(128)}, f32[32,16,128]{2,1,0:T(8,128)S(1)}, s32[32,16,128]{2,1,0:T(8,128)S(1)}, f32[32,16,256]{2,1,0:T(8,128)S(1)}, s32[]{:T(128)}) while((s32[]{:T(128)}, f32[32,16,128]{2,1,0:T(8,128)S(1)}, s32[32,16,128]{2,1,0:T(8,128)S(1)}, f32[32,16,256]{2,1,0:T(8,128)S(1)}, s32[]{:T(128)}) %tuple.63), condition=%wide.region_4.5_spmd.clone, body=%wide.region_2.4_spmd.clone.sunk | while | flops 1570818 | bytes 98377 | solution.py:77
  267.0 83.3 %all-reduce.6.cloned.1.call-done = f32[512,128]{1,0:T(8,128)} async-done(((f32[512,128]{1,0:T(8,128)}), f32[512,128]{1,0:T(8,128)}) %all-reduce.6.cloned.1.call-update) | async-done | bytes 262160 | tf_op jit(solution)/shard_map/psum | solution.py:86
  352.5 280.2 %while.23 = (s32[]{:T(128)}, f32[32,16,4096]{2,1,0:T(8,128)}, s32[32,16,128]{2,1,0:T(8,128)S(1)}, f32[32,16,128]{2,1,0:T(8,128)S(1)}, s32[]{:T(128)}) while((s32[]{:T(128)}, f32[32,16,4096]{2,1,0:T(8,128)}, s32[32,16,128]{2,1,0:T(8,128)S(1)}, f32[32,16,128]{2,1,0:T(8,128)S(1)}, s32[]{:T(128)}) %tuple.64), condition=%wide.region_9.10_spmd.clone, body=%wide.region_7.9_spmd.clone.sunk | while | flops 25100288 | bytes 836165 | solution.py:96
  361.3 8.0 select_reduce_fusion.6
  370.0 8.0 select_reduce_fusion.6
  378.8 8.0 select_reduce_fusion.6
  387.5 8.0 select_reduce_fusion.6
  396.3 8.0 select_reduce_fusion.6
  405.1 8.0 select_reduce_fusion.6
  413.8 8.0 select_reduce_fusion.6
  422.6 8.0 select_reduce_fusion.6
  431.4 8.0 select_reduce_fusion.6
  440.1 8.0 select_reduce_fusion.6
  448.9 8.0 select_reduce_fusion.6
  457.6 8.0 select_reduce_fusion.6
  466.4 8.0 select_reduce_fusion.6
  475.1 8.0 select_reduce_fusion.6
  483.9 8.0 select_reduce_fusion.6
  492.6 8.0 select_reduce_fusion.6
  501.4 8.0 select_reduce_fusion.6
  632.7 9.2 fusion.46
  642.1 65.8 %psum.29 = f32[32,32]{0,1:T(8,128)S(1)} all-reduce(f32[32,32]{0,1:T(8,128)S(1)} %fusion.36), channel_id=1, replica_groups=mesh['row'=8,'col'=16] {'row','col'}, use_global_device_ids=true, to_apply=%region_10.11 | all-reduce | flops 1024 | bytes 8192 | tf_op jit(solution)/shard_map/psum | solution.py:13
  714.8 63.7 %all_gather.10 = f32[32,4096]{0,1:T(8,128)S(1)} all-gather(f32[32,32]{0,1:T(8,128)S(1)} %fusion.23), channel_id=1, replica_groups=mesh['row'=8,'col'=16] {'row','col'}, dimensions={1}, use_global_device_ids=true | all-gather | bytes 528384 | tf_op jit(solution)/shard_map/all_gather | solution.py:17
  778.6 9.3 fusion.47
  788.1 65.0 %psum.30 = f32[32,32]{0,1:T(8,128)S(1)} all-reduce(f32[32,32]{0,1:T(8,128)S(1)} %fusion.33), channel_id=1, replica_groups=mesh['row'=8,'col'=16] {'row','col'}, use_global_device_ids=true, to_apply=%region_13.16 | all-reduce | flops 1024 | bytes 8192 | tf_op jit(solution)/shard_map/psum | solution.py:13
  860.2 65.1 %all_gather.11 = f32[32,4096]{0,1:T(8,128)S(1)} all-gather(f32[32,32]{0,1:T(8,128)S(1)} %fusion.20), channel_id=1, replica_groups=mesh['row'=8,'col'=16] {'row','col'}, dimensions={1}, use_global_device_ids=true | all-gather | bytes 528384 | tf_op jit(solution)/shard_map/all_gather | solution.py:17
  925.3 9.2 fusion.48
  934.8 65.0 %psum.31 = f32[32,32]{0,1:T(8,128)S(1)} all-reduce(f32[32,32]{0,1:T(8,128)S(1)} %fusion.29), channel_id=1, replica_groups=mesh['row'=8,'col'=16] {'row','col'}, use_global_device_ids=true, to_apply=%region_14.17 | all-reduce | flops 1024 | bytes 8192 | tf_op jit(solution)/shard_map/psum | solution.py:13
  (308 shorter events, 203.1 us)
Async XLA Ops:
  7.2 625.5 %copy-start = (f32[32,4096]{1,0:T(8,128)S(1)}, f32[32,4096]{1,0:T(8,128)}, u32[]{:S(2)}) copy-start(f32[32,4096]{1,0:T(8,128)} %param.12) | copy-start | bytes 1572868
  7.2 91.4 %all-gather.2.cloned.1.call-start = ((), (), s32[]{:S(2)}) async-start(), calls=%async_computation.1 | async-start | bytes 18874368 | tf_op jit(solution)/shard_map/all_gather | solution.py:26
  7.9 226.8 %reduce-scatter.2.cloned.1.call-start = ((), (), s32[]{:S(2)}) async-start(), calls=%async_computation.2 | async-start | bytes 6963200 | tf_op jit(solution)/shard_map/reduce_scatter | solution.py:57
  106.1 24.0 %slice-start = ((s8[16777216]{0:T(1024)(128)(4,1)}), s8[4194304]{0:T(1024)(128)(4,1)S(1)}, s32[]{:S(2)}) async-start(s8[16777216]{0:T(1024)(128)(4,1)} %bitcast.65), calls=%async_computation.4 | async-start | bytes 8388608
  108.7 21.5 %slice-start.1 = ((s8[16777216]{0:T(1024)(128)(4,1)}), s8[4194304]{0:T(1024)(128)(4,1)S(1)}, s32[]{:S(2)}) async-start(s8[16777216]{0:T(1024)(128)(4,1)} %bitcast.65), calls=%async_computation.5 | async-start | bytes 8388608
  108.7 21.4 %slice-start.2 = ((s8[16777216]{0:T(1024)(128)(4,1)}), s8[4194304]{0:T(1024)(128)(4,1)S(1)}, s32[]{:S(2)}) async-start(s8[16777216]{0:T(1024)(128)(4,1)} %bitcast.65), calls=%async_computation.6 | async-start | bytes 8388608
  108.7 21.4 %slice-start.3 = ((s8[16777216]{0:T(1024)(128)(4,1)}), s8[4194304]{0:T(1024)(128)(4,1)S(1)}, s32[]{:S(2)}) async-start(s8[16777216]{0:T(1024)(128)(4,1)} %bitcast.65), calls=%async_computation.7 | async-start | bytes 8388608
  130.1 23.9 %copy-start.1 = (s32[512,128]{1,0:T(8,128)S(1)}, s32[512,128]{1,0:T(8,128)}, u32[]{:S(2)}) copy-start(s32[512,128]{1,0:T(8,128)} %param.11) | copy-start | bytes 786436
  154.0 196.3 %all-reduce.6.cloned.1.call-start = ((), (), s32[]{:S(2)}) async-start(), calls=%async_computation.3 | async-start | bytes 524288 | tf_op jit(solution)/shard_map/psum | solution.py:86
Sparse Core Ops, SparseCore 0:
  9.7 88.8 all-gather.1
  154.1 80.6 reduce-scatter.1
  267.1 83.1 all-reduce.5
where the time goes:
time: 1020 us; the launch traced here: 1010 us
  other arithmetic  330 us (32%)
  blocking collectives  325 us (32%)
  waiting for transfers between devices  255 us (25%)
  matrix products  52.6 us (5%)
  local copies, waits for them, and re-layouts  29.2 us (3%)
  between operations  14.3 us (1%)
    reduce_sum x32, other arithmetic, operator_block(): return jnp.sum(jnp.where(match, weights[:, :, None], 0.0), axis=1)  256 us
    psum x3, blocking collectives, global_sum(): return lax.psum(value, ('row', 'col'))  196 us
    all_gather x2, blocking collectives, collect(): return lax.all_gather(columns, ('row', 'col'), axis=1, tiled=True)  129 us
    all_gather x1, waiting for transfers between devices, shards(): whole = lax.all_gather(snapshots, 'row', axis=0, tiled=True)  90.6 us
    psum x1, waiting for transfers between devices, shards(): slot_kernel = lax.psum(kernel_part, 'col')  83.3 us
    reduce_scatter x1, waiting for transfers between devices, shards(): lax.psum_scatter(jnp.where(keep, term, 0.0).astype(jnp.bfloat16), 'col',...  80.7 us
    dot_general x3, matrix products, apply_rows(): lax.dot_general(basis_rows, transition, (((1,), (1,)), ((), ())), precisi...  27.6 us
    reduce_sum x32, other arithmetic, pick_block(): return jnp.sum(jnp.where(match, lag_rows[:, None, :], 0.0), axis=2)  25.3 us
  transfers between devices with their start and end apart: 3, of which 3 were waited for; matrix products, arithmetic and copies ran while one was open for 0% of the time, Pallas kernels for 0%

commit v1 on v0

--- a/solution.py
+++ b/solution.py
@@ -23,7 +23,12 @@
     row_at = lax.axis_index("row")
     col_at = lax.axis_index("col")
     lag_count = LAGS
-    whole = lax.all_gather(snapshots, "row", axis=0, tiled=True)
+    whole = jnp.concatenate(
+        lax.all_to_all(
+            jnp.stack([snapshots for _ in range(lax.psum(1, "row"))], axis=0), "row", 0, 0
+        ),
+        0,
+    )
     snap_count = whole.shape[0]
     feat_width = whole.shape[1]
     col_block = snap_count // col_count

time: 1020 us -> 1110 us (1.088)
  waiting for transfers between devices: 255 us -> 348 us
    all_to_all x0 -> x1, waiting for transfers between devices: none -> 183 us  [shards(): lax.all_to_all(jnp.stack([snapshots for _ in range(lax.psum(1, 'row'))],...]
    all_gather x1 -> x0, waiting for transfers between devices: 90.6 us -> none  [shards(): whole = lax.all_gather(snapshots, 'row', axis=0, tiled=True)]
where the time goes in v1:
time: 1110 us; the launch traced here: 1100 us
  waiting for transfers between devices  348 us (31%)
  blocking collectives  325 us (29%)
  other arithmetic  321 us (29%)
  matrix products  50.9 us (5%)
  local copies, waits for them, and re-layouts  36 us (3%)
  between operations  14.5 us (1%)
    reduce_sum x32, other arithmetic, operator_block(): return jnp.sum(jnp.where(match, weights[:, :, None], 0.0), axis=1)  256 us
    psum x3, blocking collectives, global_sum(): return lax.psum(value, ('row', 'col'))  196 us
    all_to_all x1, waiting for transfers between devices, shards(): lax.all_to_all(jnp.stack([snapshots for _ in range(lax.psum(1, 'row'))],...  183 us
    all_gather x2, blocking collectives, collect(): return lax.all_gather(columns, ('row', 'col'), axis=1, tiled=True)  129 us
    psum x1, waiting for transfers between devices, shards(): slot_kernel = lax.psum(kernel_part, 'col')  83.3 us
    reduce_scatter x1, waiting for transfers between devices, shards(): lax.psum_scatter(jnp.where(keep, term, 0.0).astype(jnp.bfloat16), 'col',...  80.9 us
    dot_general x3, matrix products, apply_rows(): lax.dot_general(basis_rows, transition, (((1,), (1,)), ((), ())), precisi...  27.6 us
    reduce_sum x32, other arithmetic, pick_block(): return jnp.sum(jnp.where(match, lag_rows[:, None, :], 0.0), axis=2)  25.3 us
  transfers between devices with their start and end apart: 3, of which 3 were waited for; matrix products, arithmetic and copies ran while one was open for 0% of the time, Pallas kernels for 0%

profile of v1, /device:TPU:1, one launch (start us, length us, event | category | flops | bytes accessed | tf_op | source)
XLA Modules:
  0.0 1103.7 jit_solution(4570583440719818231)
XLA Ops:
  21.2 183.3 %all-to-all-done = bf16[8,512,2048]{2,1,0:T(8,128)(2,1)} async-done(((bf16[8,512,2048]{2,1,0:T(8,128)(2,1)}), bf16[8,512,2048]{2,1,0:T(8,128)(2,1)}, u32[]{:S(2)}, u32[]{:S(2)}) %all-to-all-start) | async-done | bytes 16777248 | tf_op jit(solution)/shard_map/all_to_all | solution.py:27
  214.4 13.2 %fusion.5 = bf16[16,320,2048]{2,1,0:T(8,128)(2,1)S(1)} fusion(bf16[15,64,2048]{2,1,0:T(8,128)(2,1)S(1)} %slice.69, bf16[16,256,2048]{2,1,0:T(8,128)(2,1)} %bitcast.2), kind=kLoop, calls=%fused_computation.15 | loop fusion | flops 62914560 | bytes 41680896 | tf_op jit(solution)/shard_map/concatenate | solution.py:49
  227.7 22.2 %select_convert_fusion = bf16[5120,576]{1,0:T(8,128)(2,1)} fusion(bf16[5120,2048]{1,0:T(8,128)(2,1)S(1)} %bitcast.69, f32[576]{0:T(1024)S(1)} %pad_dynamic-slice_fusion.2, f32[5120]{0:T(1024)S(1)} %add.130, pred[576]{0:T(1024)(128)(4,1)S(1)} %add_compare_fusion, pred[5120]{0:T(1024)(128)(4,1)S(1)} %fusion.17, s32[]{:T(128)S(6)} %select_n.56, ...), kind=kOutput, calls=%fused_computation.17 | convolution fusion | flops 12097290240 | bytes 43675460 | tf_op jit(solution)/shard_map/dot_general | solution.py:57
  250.0 80.9 %reduce-scatter.2.cloned.1.call-done = bf16[320,576]{1,0:T(8,128)(2,1)} async-done(((bf16[5120,576]{1,0:T(8,128)(2,1)}), bf16[320,576]{1,0:T(8,128)(2,1)}) %reduce-scatter.2.cloned.1.call-update) | async-done | bytes 368656 | tf_op jit(solution)/shard_map/reduce_scatter | solution.py:62
  334.3 28.1 %while.22 = (s32[]{:T(128)}, f32[32,16,128]{2,1,0:T(8,128)S(1)}, s32[32,16,128]{2,1,0:T(8,128)S(1)}, f32[32,16,256]{2,1,0:T(8,128)S(1)}, s32[]{:T(128)}) while((s32[]{:T(128)}, f32[32,16,128]{2,1,0:T(8,128)S(1)}, s32[32,16,128]{2,1,0:T(8,128)S(1)}, f32[32,16,256]{2,1,0:T(8,128)S(1)}, s32[]{:T(128)}) %tuple.61), condition=%wide.region_4.5_spmd.clone, body=%wide.region_2.4_spmd.clone.sunk | while | flops 1570818 | bytes 98377 | solution.py:82
  363.2 83.3 %all-reduce.6.cloned.1.call-done = f32[512,128]{1,0:T(8,128)} async-done(((f32[512,128]{1,0:T(8,128)}), f32[512,128]{1,0:T(8,128)}) %all-reduce.6.cloned.1.call-update) | async-done | bytes 262160 | tf_op jit(solution)/shard_map/psum | solution.py:91
  448.7 279.5 %while.23 = (s32[]{:T(128)}, f32[32,16,4096]{2,1,0:T(8,128)}, s32[32,16,128]{2,1,0:T(8,128)S(1)}, f32[32,16,128]{2,1,0:T(8,128)S(1)}, s32[]{:T(128)}) while((s32[]{:T(128)}, f32[32,16,4096]{2,1,0:T(8,128)}, s32[32,16,128]{2,1,0:T(8,128)S(1)}, f32[32,16,128]{2,1,0:T(8,128)S(1)}, s32[]{:T(128)}) %tuple.62), condition=%wide.region_9.10_spmd.clone, body=%wide.region_7.9_spmd.clone.sunk | while | flops 25100288 | bytes 836165 | solution.py:101
  457.5 8.0 select_reduce_fusion.6
  474.9 8.0 select_reduce_fusion.6
  483.7 8.0 select_reduce_fusion.6
  509.9 8.0 select_reduce_fusion.6
  518.6 8.0 select_reduce_fusion.6
  527.4 8.0 select_reduce_fusion.6
  544.8 8.0 select_reduce_fusion.6
  553.6 8.0 select_reduce_fusion.6
  562.3 8.0 select_reduce_fusion.6
  571.0 8.0 select_reduce_fusion.6
  597.2 8.0 select_reduce_fusion.6
  632.2 8.0 select_reduce_fusion.6
  640.9 8.0 select_reduce_fusion.6
  649.6 8.0 select_reduce_fusion.6
  658.4 8.0 select_reduce_fusion.6
  667.1 8.0 select_reduce_fusion.6
  675.9 8.0 select_reduce_fusion.6
  728.2 9.2 fusion.46
  737.6 65.8 %psum.29 = f32[32,32]{0,1:T(8,128)S(1)} all-reduce(f32[32,32]{0,1:T(8,128)S(1)} %fusion.36), channel_id=1, replica_groups=mesh['row'=8,'col'=16] {'row','col'}, use_global_device_ids=true, to_apply=%region_10.11 | all-reduce | flops 1024 | bytes 8192 | tf_op jit(solution)/shard_map/psum | solution.py:13
  810.4 63.7 %all_gather.6 = f32[32,4096]{0,1:T(8,128)S(1)} all-gather(f32[32,32]{0,1:T(8,128)S(1)} %fusion.23), channel_id=1, replica_groups=mesh['row'=8,'col'=16] {'row','col'}, dimensions={1}, use_global_device_ids=true | all-gather | bytes 528384 | tf_op jit(solution)/shard_map/all_gather | solution.py:17
  874.1 9.3 fusion.47
  883.6 65.0 %psum.30 = f32[32,32]{0,1:T(8,128)S(1)} all-reduce(f32[32,32]{0,1:T(8,128)S(1)} %fusion.33), channel_id=1, replica_groups=mesh['row'=8,'col'=16] {'row','col'}, use_global_device_ids=true, to_apply=%region_13.16 | all-reduce | flops 1024 | bytes 8192 | tf_op jit(solution)/shard_map/psum | solution.py:13
  955.7 65.1 %all_gather.7 = f32[32,4096]{0,1:T(8,128)S(1)} all-gather(f32[32,32]{0,1:T(8,128)S(1)} %fusion.20), channel_id=1, replica_groups=mesh['row'=8,'col'=16] {'row','col'}, dimensions={1}, use_global_device_ids=true | all-gather | bytes 528384 | tf_op jit(solution)/shard_map/all_gather | solution.py:17
  1020.8 9.2 fusion.48
  1030.3 65.0 %psum.31 = f32[32,32]{0,1:T(8,128)S(1)} all-reduce(f32[32,32]{0,1:T(8,128)S(1)} %fusion.29), channel_id=1, replica_groups=mesh['row'=8,'col'=16] {'row','col'}, use_global_device_ids=true, to_apply=%region_14.17 | all-reduce | flops 1024 | bytes 8192 | tf_op jit(solution)/shard_map/psum | solution.py:13
  (300 shorter events, 215.9 us)
Async XLA Ops:
  7.2 721.1 %copy-start = (f32[32,4096]{1,0:T(8,128)S(1)}, f32[32,4096]{1,0:T(8,128)}, u32[]{:S(2)}) copy-start(f32[32,4096]{1,0:T(8,128)} %param.12) | copy-start | bytes 1572868
  14.1 190.4 %all-to-all-start = ((bf16[8,512,2048]{2,1,0:T(8,128)(2,1)}), bf16[8,512,2048]{2,1,0:T(8,128)(2,1)}, u32[]{:S(2)}, u32[]{:S(2)}) async-start(bf16[8,512,2048]{2,1,0:T(8,128)(2,1)} %stack.2), calls=%async_computation | async-start | bytes 33554432 | tf_op jit(solution)/shard_map/all_to_all | solution.py:27
  21.2 309.8 %reduce-scatter.2.cloned.1.call-start = ((), (), s32[]{:S(2)}) async-start(), calls=%async_computation.2 | async-start | bytes 6963200 | tf_op jit(solution)/shard_map/reduce_scatter | solution.py:62
  227.7 22.3 %copy-start.1 = (s32[512,128]{1,0:T(8,128)S(1)}, s32[512,128]{1,0:T(8,128)}, u32[]{:S(2)}) copy-start(s32[512,128]{1,0:T(8,128)} %param.11) | copy-start | bytes 786436
  249.9 196.6 %all-reduce.6.cloned.1.call-start = ((), (), s32[]{:S(2)}) async-start(), calls=%async_computation.3 | async-start | bytes 524288 | tf_op jit(solution)/shard_map/psum | solution.py:91
Sparse Core Ops, SparseCore 0:
  250.0 80.8 reduce-scatter.1
  363.3 83.1 all-reduce.5
